TPU v7x, 32 devices: a whole 2x2x4 slice. The times are simulated.
32 devices in a mesh: groups: 2 (over x), ctx: 16 (over z, y, core).
Axes of the slice: x: 2, y: 2, z: 4, core: 2. Of those that a mesh axis runs over, the one named last changes fastest.
Arguments:
- context_keys: bfloat16 [4096, 2048], P(('groups', 'ctx')), parts along dimension 0, may hold values from -6 to 6
- context_values: bfloat16 [4096, 2048], P(('groups', 'ctx')), parts along dimension 0, may hold values from -6 to 6
- context_queries: bfloat16 [4096, 2048], P(('groups', 'ctx')), parts along dimension 0, may hold values from -6 to 6
- token_rates: float32 [8, 4096], P(None, ('groups', 'ctx')), parts along dimension 1, may hold values from 0.05 to 1
- w_gate: bfloat16 [8, 256, 256], replicated, may hold values from -0.375 to 0.375
- w_up: bfloat16 [8, 256, 256], replicated, may hold values from -0.375 to 0.375
- w_down: bfloat16 [8, 256, 256], replicated, may hold values from -0.375 to 0.375
- question_rows: bfloat16 [8192, 2048], P(('groups', 'ctx')), parts along dimension 0, may hold values from -6 to 6
- question_count: int32 [32], P(('groups', 'ctx')), parts along dimension 0, may hold values from 1 to 256, 1024 in all
Outputs:
- context_out: bfloat16 [4096, 2048], P(('groups', 'ctx')), parts along dimension 0
- answers: bfloat16 [8192, 2048], P(('groups', 'ctx')), parts along dimension 0
There are 2 independent parts, one for each index of `groups`. A program takes and returns all parts, laid end to end along the dimension named above; an argument that names none is the same for every part. Nothing has to cross between parts.
Inputs may be any that keep to these rules, and one draw needn't show every extreme that they name: `question_count`: live rows are the first of each device's 256 slots. The counts of one user (the devices along ctx) add up to exactly 1024, and some device of each user has exactly 256.
All inputs are finite; a program needn't handle non-finite values.
Results may differ from a plain program's by a relative error of at most 0.018.
Values may be sent and summed in bfloat16 or wider, within the bound.
A program may use at most 128 MiB of HBM per device.

v0:
```python
import jax
import jax.numpy as jnp
from jax import lax
from jax.sharding import PartitionSpec as P

NS_STEPS = 3
quintic_first = 3.4445
quintic_second = -4.775
quintic_third = 2.0315


def fast_apply(in_rows, w_gate, w_up, w_down):
    head_count = w_gate.shape[0]
    head_size = w_gate.shape[1]
    row_split = in_rows.reshape(in_rows.shape[0], head_count, head_size)
    pre_gate = jnp.einsum("thd,hde->hte", row_split, w_gate, preferred_element_type=jnp.float32)
    pre_up = jnp.einsum("thd,hde->hte", row_split, w_up, preferred_element_type=jnp.float32)
    hidden = (jax.nn.silu(pre_gate) * pre_up).astype(jnp.bfloat16)
    outputs = jnp.einsum("hte,hef->thf", hidden, w_down, preferred_element_type=jnp.float32)
    return outputs.reshape(in_rows.shape[0], head_count * head_size).astype(jnp.bfloat16)


def directions(context_keys, context_values, token_rates, w_gate, w_up, w_down):
    tok_rows = context_keys.shape[0]
    head_count = w_gate.shape[0]
    head_size = w_gate.shape[1]
    key_split = context_keys.reshape(tok_rows, head_count, head_size)
    value_split = context_values.reshape(tok_rows, head_count, head_size)
    pre_gate = jnp.einsum("thd,hde->hte", key_split, w_gate, preferred_element_type=jnp.float32)
    pre_up = jnp.einsum("thd,hde->hte", key_split, w_up, preferred_element_type=jnp.float32)
    sigmoid_gate = jax.nn.sigmoid(pre_gate)
    activated = pre_gate * sigmoid_gate
    hidden = (activated * pre_up).astype(jnp.bfloat16)
    weighted = (token_rates.T[:, :, None] * value_split).astype(jnp.bfloat16)
    back_hidden = jnp.einsum("thf,hef->hte", weighted, w_down, preferred_element_type=jnp.float32)
    back_gate = (
        back_hidden * pre_up * sigmoid_gate * (1.0 + pre_gate * (1.0 - sigmoid_gate))
    ).astype(jnp.bfloat16)
    back_up = (back_hidden * activated).astype(jnp.bfloat16)
    step_gate = jnp.einsum("thd,hte->hde", key_split, back_gate, preferred_element_type=jnp.float32)
    step_up = jnp.einsum("thd,hte->hde", key_split, back_up, preferred_element_type=jnp.float32)
    step_down = jnp.einsum("hte,thf->hef", hidden, weighted, preferred_element_type=jnp.float32)
    return jnp.stack([step_gate, step_up, step_down])


def per_device(
    context_keys,
    context_values,
    context_queries,
    token_rates,
    w_gate,
    w_up,
    w_down,
    question_rows,
    question_count,
):
    head_count = w_gate.shape[0]
    head_size = w_gate.shape[1]
    matrix_count = 3 * head_count
    context_out = fast_apply(context_queries, w_gate, w_up, w_down)
    direction = directions(context_keys, context_values, token_rates, w_gate, w_up, w_down)
    flat_grads = direction.reshape(matrix_count, head_size * head_size)
    total = lax.psum(flat_grads, "ctx")
    norm_sizes = jnp.sqrt(jnp.sum(total * total, axis=1, keepdims=True))
    scaled = (total / (norm_sizes + 1e-06)).astype(jnp.bfloat16)
    iterate = scaled.reshape(matrix_count, head_size, head_size)
    for sweep_index in range(NS_STEPS):
        gram_matrix = jnp.einsum(
            "mij,mkj->mik", iterate, iterate, preferred_element_type=jnp.float32
        ).astype(jnp.bfloat16)
        gram_square = jnp.einsum(
            "mij,mjk->mik", gram_matrix, gram_matrix, preferred_element_type=jnp.float32
        )
        polynomial = (
            quintic_second * gram_matrix.astype(jnp.float32) + quintic_third * gram_square
        ).astype(jnp.bfloat16)
        product = jnp.einsum(
            "mij,mjk->mik", polynomial, iterate, preferred_element_type=jnp.float32
        )
        iterate = (quintic_first * iterate.astype(jnp.float32) + product).astype(jnp.bfloat16)
    previous = jnp.stack([w_gate, w_up, w_down]).astype(jnp.float32)
    moved = previous + iterate.reshape(3, head_count, head_size, head_size).astype(jnp.float32)
    col_norms = jnp.sqrt(jnp.sum(previous * previous, axis=2, keepdims=True))
    updated = (
        moved * col_norms / jnp.sqrt(jnp.sum(moved * moved, axis=2, keepdims=True) + 1e-06)
    ).astype(jnp.bfloat16)
    capacity = question_rows.shape[0]
    outputs = fast_apply(question_rows, updated[0], updated[1], updated[2])
    live_mask = jnp.arange(capacity, dtype=jnp.int32) < question_count[0]
    answers = jnp.where(live_mask[:, None], outputs, jnp.zeros_like(outputs))
    return (context_out, answers)


def solution(mesh):
    return jax.shard_map(
        per_device,
        mesh=mesh,
        in_specs=(
            P(("groups", "ctx"), None),
            P(("groups", "ctx"), None),
            P(("groups", "ctx"), None),
            P(None, ("groups", "ctx")),
            P(),
            P(),
            P(),
            P(("groups", "ctx"), None),
            P(("groups", "ctx")),
        ),
        out_specs=(P(("groups", "ctx"), None), P(("groups", "ctx"), None)),
        check_vma=False,
    )
```

profile of v0, /device:TPU:0, one launch (start us, length us, event | category | flops | bytes accessed | tf_op | source)
XLA Modules:
  0.0 236.1 jit_solution(8442899116746412055)
XLA Ops:
  7.2 0.0 copy-start.11
  7.2 0.0 copy-start.16
  7.2 0.0 all-reduce.2.cloned.1.call-start
  7.2 0.0 copy-start.9
  7.2 0.0 copy-start.17
  7.3 1.8 fusion.41
  9.1 0.0 copy-done.11
  9.1 1.4 fusion.43
  10.5 0.0 copy-done.16
  10.5 0.1 convert_element_type.148
  10.6 0.0 copy-done.9
  10.6 0.0 copy-done.17
  10.6 0.5 fusion.61
  11.1 0.0 copy-start.15
  11.1 0.7 convolution_bitcast_fusion
  11.8 0.4 copy-done.15
  12.1 0.6 convolution_bitcast_fusion.2
  12.8 0.6 convolution_bitcast_fusion.1
  13.4 3.3 %pad_maximum_fusion = f32[3,8,256,256]{2,3,1,0:T(8,128)} fusion(f32[1,8,256,256]{2,3,1,0:T(8,128)S(1)} %convolution_bitcast_fusion, f32[1,8,256,256]{2,3,1,0:T(8,128)S(1)} %convolution_bitcast_fusion.1, f32[1,8,256,256]{2,3,1,0:T(8,128)S(1)} %convolution_bitcast_fusion.2), kind=kLoop, calls=%fused_computation | loop fusion | flops 3145728 | bytes 12582912 | tf_op jit(solution)/shard_map/stack | solution.py:43
  16.7 6.7 %copy.60 = f32[3,8,256,256]{3,1,2,0:T(8,128)} copy(f32[3,8,256,256]{2,3,1,0:T(8,128)} %pad_maximum_fusion) | data formatting | bytes 12582912
  23.4 0.0 all-reduce.2.cloned.1.call-update
  23.4 1.2 copy-done.7
  24.6 0.5 copy.31
  25.1 0.0 copy-start.1
  25.1 0.5 copy.32
  25.6 0.0 copy-start.3
  25.7 1.9 copy.33
  27.5 0.0 copy-start.5
  27.5 3.1 %maximum_convert_fusion = f32[3,8,256,256]{2,3,1,0:T(8,128)} fusion(bf16[1,8,256,256]{2,3,1,0:T(8,128)(2,1)S(1)} %bitcast.124, bf16[1,8,256,256]{2,3,1,0:T(8,128)(2,1)S(1)} %bitcast.121, bf16[1,8,256,256]{2,3,1,0:T(8,128)(2,1)S(1)} %bitcast.118), kind=kLoop, calls=%fused_computation.18 | loop fusion | flops 4718592 | bytes 9437184 | tf_op jit(solution)/shard_map/convert_element_type | solution.py:81
  30.6 7.0 %copy.45 = f32[3,8,256,256]{3,2,1,0:T(8,128)} copy(f32[3,8,256,256]{2,3,1,0:T(8,128)} %maximum_convert_fusion) | data formatting | bytes 12582912 | tf_op jit(solution)/shard_map/convert_element_type | solution.py:81
  37.6 0.0 copy-done.1
  37.6 0.0 copy-done.3
  37.6 0.0 copy-done.5
  37.6 1.0 multiply_reduce_fusion
  38.6 0.0 copy-start.10
  38.6 0.0 copy-start.12
  38.6 2.4 %copy.56 = bf16[256,2048]{0,1:T(8,128)(2,1)} copy(bf16[256,2048]{1,0:T(8,128)(2,1)} %param.16) | data formatting | bytes 2097152 | tf_op jit(solution)/shard_map/reshape | solution.py:15
  41.7 1.7 fusion.47
  43.4 0.0 copy-done.10
  43.4 0.0 copy-done.12
  43.4 2.5 %fusion.29 = bf16[128,8,256]{2,0,1:T(8,128)(2,1)} fusion(bf16[8,256,256]{2,1,0:T(8,128)(2,1)S(1)} %copy-done.10, bf16[8,256,256]{2,1,0:T(8,128)(2,1)S(1)} %copy-done.12, f32[8,128,256]{2,1,0:T(8,128)S(1)} %fusion.47, bf16[16,8,8,256]{3,2,1,0:T(8,128)(2,1)} %bitcast.140), kind=kOutput, calls=%fused_computation.45 | convolution fusion | flops 270270464 | bytes 4194304 | tf_op jit(solution)/shard_map/hte,hef->thf/dot_general | solution.py:19
  45.9 1.3 copy.30
  47.2 1.0 copy.49
  48.3 117.3 %all-reduce.2.cloned.1.call-done = f32[24,65536]{1,0:T(8,128)} async-done(((f32[24,65536]{1,0:T(8,128)}), f32[24,65536]{1,0:T(8,128)}) %all-reduce.2.cloned.1.call-update) | async-done | bytes 6291472 | tf_op jit(solution)/shard_map/psum | solution.py:63
  165.5 3.6 %multiply_reduce_fusion.1 = f32[24]{0:T(128)S(1)} fusion(f32[24,65536]{1,0:T(8,128)} %all-reduce.2.cloned.1.call-done), kind=kLoop, calls=%fused_computation.13 | loop fusion | flops 3145704 | bytes 6291552 | tf_op jit(solution)/shard_map/reduce_sum | solution.py:64
  169.1 1.0 copy-done
  170.1 0.4 divide_convert_fusion.1
  170.5 0.7 copy.61
  171.3 2.7 %fusion.74 = bf16[24,256,256]{2,1,0:T(8,128)(2,1)} fusion(bf16[24,256,256]{2,1,0:T(8,128)(2,1)S(1)} %bitcast.115), kind=kOutput, calls=%fused_computation.96 | convolution fusion | flops 805306368 | bytes 6291456 | tf_op jit(solution)/shard_map/mij,mkj->mik/dot_general | solution.py:68
  173.9 7.8 %add_convert_fusion.4 = bf16[24,256,256]{2,1,0:T(8,128)(2,1)} fusion(bf16[24,256,256]{2,1,0:T(8,128)(2,1)S(1)} %bitcast.116, bf16[24,256,256]{2,1,0:T(8,128)(2,1)} %fusion.74), kind=kOutput, calls=%fused_computation.10 | convolution fusion | flops 1624768512 | bytes 9437184 | tf_op jit(solution)/shard_map/mij,mjk->mik/dot_general | solution.py:77
  181.8 5.5 %fusion.75 = bf16[24,256,256]{2,1,0:T(8,128)(2,1)} fusion(bf16[24,256,256]{2,1,0:T(8,128)(2,1)} %add_convert_fusion.4), kind=kOutput, calls=%fused_computation.97 | convolution fusion | flops 805306368 | bytes 6291456 | tf_op jit(solution)/shard_map/mij,mkj->mik/dot_general | solution.py:68
  187.3 8.2 %add_convert_fusion.2 = bf16[24,256,256]{2,1,0:T(8,128)(2,1)S(1)} fusion(bf16[24,256,256]{2,1,0:T(8,128)(2,1)} %add_convert_fusion.4, bf16[24,256,256]{2,1,0:T(8,128)(2,1)} %fusion.75), kind=kOutput, calls=%fused_computation.8 | convolution fusion | flops 1624768512 | bytes 9437184 | tf_op jit(solution)/shard_map/mij,mjk->mik/dot_general | solution.py:77
  195.5 2.7 %fusion.76 = bf16[24,256,256]{2,1,0:T(8,128)(2,1)} fusion(bf16[24,256,256]{2,1,0:T(8,128)(2,1)S(1)} %add_convert_fusion.2), kind=kOutput, calls=%fused_computation.98 | convolution fusion | flops 805306368 | bytes 6291456 | tf_op jit(solution)/shard_map/mij,mkj->mik/dot_general | solution.py:68
  198.1 11.6 %fusion.1 = (f32[24,256]{1,0:T(8,128)S(1)}, f32[24,256,256]{2,1,0:T(8,128)}) fusion(f32[3,8,256,256]{3,2,1,0:T(8,128)} %copy.45, bf16[24,256,256]{2,1,0:T(8,128)(2,1)S(1)} %add_convert_fusion.2, bf16[24,256,256]{2,1,0:T(8,128)(2,1)} %fusion.76), kind=kOutput, calls=%fused_computation.3 | convolution fusion | flops 1631053824 | bytes 18898944 | tf_op jit(solution)/shard_map/mij,mjk->mik/dot_general | solution.py:77
  209.7 6.7 %copy.44 = f32[3,8,256,256]{2,3,1,0:T(8,128)} copy(f32[3,8,256,256]{3,2,1,0:T(8,128)} %bitcast.128) | data formatting | bytes 12582912 | tf_op jit(solution)/shard_map/convert_element_type | solution.py:82
  216.5 0.0 copy-start.13
  216.5 4.6 %divide_convert_fusion = bf16[3,8,256,256]{2,3,1,0:T(8,128)(2,1)S(1)} fusion(f32[3,8,256,256]{2,3,1,0:T(8,128)} %copy.44, f32[3,8,256]{2,1,0:T(8,128)S(1)} %sqrt_bitcast_fusion, f32[3,8,256]{2,1,0:T(8,128)S(1)} %sqrt.28, bf16[1,8,256,256]{2,3,1,0:T(8,128)(2,1)S(1)} %bitcast.126, bf16[1,8,256,256]{2,3,1,0:T(8,128)(2,1)S(1)} %bitcast.123, ...), kind=kLoop, calls=%fused_computation.4 | loop fusion | flops 11010048 | bytes 12632064 | tf_op jit(solution)/shard_map/convert_element_type | solution.py:86
  221.1 0.0 copy-start.14
  221.1 1.6 copy-done.8
  222.7 0.4 fusion.31
  223.1 0.0 copy-done.14
  223.1 3.5 %convolution_convert_fusion = bf16[8,256,256]{2,1,0:T(8,128)(2,1)} fusion(f32[8,256,256]{2,1,0:T(8,128)S(1)} %fusion.31, bf16[256,8,256]{0,2,1:T(8,128)(2,1)S(1)} %bitcast.132, bf16[3,8,256,256]{2,3,1,0:T(8,128)(2,1)} %copy-done.8), kind=kOutput, calls=%fused_computation.41 | convolution fusion | flops 540540928 | bytes 6291456 | tf_op jit(solution)/shard_map/hte,hef->thf/dot_general | solution.py:19
  226.7 1.5 copy.48
  228.2 1.1 broadcast_select_fusion
  (14 shorter events, 0.1 us)
Async XLA Ops:
  7.2 1.9 copy-start.11
  7.2 3.3 %copy-start.16 = (bf16[128,2048]{1,0:T(8,128)(2,1)S(1)}, bf16[128,2048]{1,0:T(8,128)(2,1)}, u32[]{:S(2)}) copy-start(bf16[128,2048]{1,0:T(8,128)(2,1)} %param.10) | copy-start | bytes 1572868
  7.2 158.3 %all-reduce.2.cloned.1.call-start = ((), (), s32[]{:S(2)}) async-start(), calls=%async_computation | async-start | bytes 12582912 | tf_op jit(solution)/shard_map/psum | solution.py:63
  7.2 3.4 %copy-start.9 = (bf16[8,256,256]{2,1,0:T(8,128)(2,1)S(1)}, bf16[8,256,256]{2,1,0:T(8,128)(2,1)}, u32[]{:S(2)}) copy-start(bf16[8,256,256]{2,1,0:T(8,128)(2,1)} %param.15) | copy-start | bytes 3145732
  7.2 3.3 %copy-start.17 = (f32[8,128]{1,0:T(8,128)S(1)}, f32[8,128]{1,0:T(8,128)}, u32[]{:S(2)}) copy-start(f32[8,128]{1,0:T(8,128)} %param.12) | copy-start | bytes 12292
  11.1 1.0 copy-start.15
  23.4 1.2 copy-start.7
  25.1 12.5 %copy-start.1 = (bf16[8,256,256]{1,2,0:T(8,128)(2,1)}, bf16[8,256,256]{1,2,0:T(8,128)(2,1)S(1)}, u32[]{:S(2)}) copy-start(bf16[8,256,256]{1,2,0:T(8,128)(2,1)S(1)} %copy.31) | copy-start | bytes 3145732
  25.6 11.9 %copy-start.3 = (bf16[8,256,256]{1,2,0:T(8,128)(2,1)}, bf16[8,256,256]{1,2,0:T(8,128)(2,1)S(1)}, u32[]{:S(2)}) copy-start(bf16[8,256,256]{1,2,0:T(8,128)(2,1)S(1)} %copy.32) | copy-start | bytes 3145732
  27.5 10.1 %copy-start.5 = (bf16[8,256,256]{1,2,0:T(8,128)(2,1)}, bf16[8,256,256]{1,2,0:T(8,128)(2,1)S(1)}, u32[]{:S(2)}) copy-start(bf16[8,256,256]{1,2,0:T(8,128)(2,1)S(1)} %copy.33) | copy-start | bytes 3145732
  38.6 4.8 %copy-start.10 = (bf16[8,256,256]{2,1,0:T(8,128)(2,1)S(1)}, bf16[8,256,256]{2,1,0:T(8,128)(2,1)}, u32[]{:S(2)}) copy-start(bf16[8,256,256]{2,1,0:T(8,128)(2,1)} %param.15) | copy-start | bytes 3145732
  38.6 4.8 %copy-start.12 = (bf16[8,256,256]{2,1,0:T(8,128)(2,1)S(1)}, bf16[8,256,256]{2,1,0:T(8,128)(2,1)}, u32[]{:S(2)}) copy-start(bf16[8,256,256]{2,1,0:T(8,128)(2,1)} %param.14) | copy-start | bytes 3145732
  165.5 4.6 %copy-start = (f32[24,65536]{1,0:T(8,128)S(1)}, f32[24,65536]{1,0:T(8,128)}, u32[]{:S(2)}) copy-start(f32[24,65536]{1,0:T(8,128)} %all-reduce.2.cloned.1.call-done) | copy-start | bytes 18874372
  209.7 6.7 %copy-start.2 = (bf16[8,256,256]{1,2,0:T(8,128)(2,1)S(1)}, bf16[8,256,256]{1,2,0:T(8,128)(2,1)}, u32[]{:S(2)}) copy-start(bf16[8,256,256]{1,2,0:T(8,128)(2,1)} %copy-done.1) | copy-start | bytes 3145732
  209.7 6.7 %copy-start.4 = (bf16[8,256,256]{1,2,0:T(8,128)(2,1)S(1)}, bf16[8,256,256]{1,2,0:T(8,128)(2,1)}, u32[]{:S(2)}) copy-start(bf16[8,256,256]{1,2,0:T(8,128)(2,1)} %copy-done.3) | copy-start | bytes 3145732
  209.7 6.7 %copy-start.6 = (bf16[8,256,256]{1,2,0:T(8,128)(2,1)S(1)}, bf16[8,256,256]{1,2,0:T(8,128)(2,1)}, u32[]{:S(2)}) copy-start(bf16[8,256,256]{1,2,0:T(8,128)(2,1)} %copy-done.5) | copy-start | bytes 3145732
  216.5 6.2 %copy-start.13 = (bf16[256,2048]{0,1:T(8,128)(2,1)S(1)}, bf16[256,2048]{0,1:T(8,128)(2,1)}, u32[]{:S(2)}) copy-start(bf16[256,2048]{0,1:T(8,128)(2,1)} %copy.56) | copy-start | bytes 3145732
  221.1 1.6 copy-start.8
  221.1 2.1 copy-start.14
Sparse Core Ops, SparseCore 0:
  23.5 141.9 all-reduce.1
where the time goes:
time: 237 us; the launch traced here: 236 us
  waiting for transfers between devices  117 us (49%)
  matrix products  52.2 us (22%)
  local copies, waits for them, and re-layouts  34.4 us (15%)
  other arithmetic  17.2 us (7%)
  between operations  15 us (6%)
    psum x1, waiting for transfers between devices, per_device(): total = lax.psum(flat_grads, 'ctx')  117 us
    dot_general x3, matrix products, per_device(): jnp.einsum('mij,mjk->mik', polynomial, iterate, preferred_element_type=jn...  27.6 us
    unnamed x42, local copies, waits for them, and re-layouts  15.6 us
    dot_general x3, matrix products, per_device(): jnp.einsum('mij,mkj->mik', iterate, iterate, preferred_element_type=jnp.f...  10.9 us
    convert_element_type x1, local copies, waits for them, and re-layouts, per_device(): previous = jnp.stack([w_gate, w_up, w_down]).astype(jnp.float32)  6.96 us
    convert_element_type x1, local copies, waits for them, and re-layouts, per_device(): iterate.reshape(3, head_count, head_size, head_size).astype(jnp.float32)  6.7 us
    dot_general x2, matrix products, fast_apply(): jnp.einsum('hte,hef->thf', hidden, w_down, preferred_element_type=jnp.flo...  6.01 us
  transfers between devices with their start and end apart: 1, of which 1 were waited for; matrix products, arithmetic and copies ran while one was open for 10% of the time, Pallas kernels for 0%

commit v1 on v0

--- a/solution.py
+++ b/solution.py
@@ -60,7 +60,9 @@
     context_out = fast_apply(context_queries, w_gate, w_up, w_down)
     direction = directions(context_keys, context_values, token_rates, w_gate, w_up, w_down)
     flat_grads = direction.reshape(matrix_count, head_size * head_size)
-    total = lax.psum(flat_grads, "ctx")
+    total = flat_grads
+    for hop in (1, 2, 4, 8):
+        total = total + lax.ppermute(total, "ctx", [(dev, dev ^ hop) for dev in range(16)])
     norm_sizes = jnp.sqrt(jnp.sum(total * total, axis=1, keepdims=True))
     scaled = (total / (norm_sizes + 1e-06)).astype(jnp.bfloat16)
     iterate = scaled.reshape(matrix_count, head_size, head_size)

time: 237 us -> 648 us (2.73)
  waiting for transfers between devices: 117 us -> 527 us
  between operations: 15 us -> 1.64 us
  other arithmetic: 17.2 us -> 26.5 us
  starting transfers between devices: 0.04 us -> 7.83 us
    ppermute x0 -> x4, waiting for transfers between devices: none -> 527 us  [per_device(): lax.ppermute(total, 'ctx', [(dev, dev ^ hop) for dev in range(16)])]
    psum x1 -> x0, waiting for transfers between devices: 117 us -> none  [per_device(): total = lax.psum(flat_grads, 'ctx')]
    ppermute x0 -> x4, starting transfers between devices: none -> 7.83 us  [per_device(): lax.ppermute(total, 'ctx', [(dev, dev ^ hop) for dev in range(16)])]
    add x0 -> x3, other arithmetic: none -> 7.5 us  [per_device(): total + lax.ppermute(total, 'ctx', [(dev, dev ^ hop) for dev in range(16)])]
  transfers between devices with their start and end apart: 1 -> 4, of which waited for: 1 -> 4; matrix products, arithmetic and copies ran while one was open for 10% -> 3% of each run, Pallas kernels for 0% -> 0%
where the time goes in v1:
time: 648 us; the launch traced here: 647 us
  waiting for transfers between devices  527 us (81%)
  matrix products  52.3 us (8%)
  local copies, waits for them, and re-layouts  31.9 us (5%)
  other arithmetic  26.5 us (4%)
  starting transfers between devices  7.83 us (1%)
    ppermute x4, waiting for transfers between devices, per_device(): lax.ppermute(total, 'ctx', [(dev, dev ^ hop) for dev in range(16)])  527 us
    dot_general x3, matrix products, per_device(): jnp.einsum('mij,mjk->mik', polynomial, iterate, preferred_element_type=jn...  27.7 us
    unnamed x42, local copies, waits for them, and re-layouts  13.4 us
  transfers between devices with their start and end apart: 4, of which 4 were waited for; matrix products, arithmetic and copies ran while one was open for 3% of the time, Pallas kernels for 0%

profile of v1, /device:TPU:0, one launch (start us, length us, event | category | flops | bytes accessed | tf_op | source)
XLA Modules:
  0.0 647.5 jit_solution(11645522770556598835)
XLA Ops:
  0.6 0.0 copy-start.10
  0.6 0.0 copy-start.16
  0.7 0.0 copy-start.8
  0.7 0.0 copy-start.17
  0.7 1.8 fusion.41
  2.5 0.0 copy-done.10
  2.5 1.4 fusion.43
  3.9 0.0 copy-done.16
  3.9 0.1 convert_element_type.148
  4.0 0.5 fusion.61
  4.5 0.0 copy-start.15
  4.5 0.7 convolution_bitcast_fusion
  5.2 0.4 copy-done.15
  5.6 0.6 convolution_bitcast_fusion.2
  6.2 0.6 convolution_bitcast_fusion.1
  6.8 3.3 pad_maximum_fusion
  10.1 6.7 %copy.60 = f32[3,8,256,256]{3,1,2,0:T(8,128)} copy(f32[3,8,256,256]{2,3,1,0:T(8,128)} %pad_maximum_fusion) | data formatting | bytes 12582912
  16.8 0.5 collective-permute-start
  17.3 10.0 %collective-permute-done = f32[24,65536]{1,0:T(8,128)S(1)} collective-permute-done((f32[24,65536]{1,0:T(8,128)}, f32[24,65536]{1,0:T(8,128)S(1)}, u32[]{:S(2)}, u32[]{:S(2)}) %collective-permute-start) | collective-permute-done | bytes 6291488 | tf_op jit(solution)/shard_map/ppermute | solution.py:65
  27.3 3.6 add.73
  30.9 2.9 collective-permute-start.1
  33.8 135.8 %collective-permute-done.1 = f32[24,65536]{1,0:T(8,128)S(1)} collective-permute-done((f32[24,65536]{1,0:T(8,128)S(1)}, f32[24,65536]{1,0:T(8,128)S(1)}, u32[]{:S(2)}, u32[]{:S(2)}) %collective-permute-start.1) | collective-permute-done | bytes 6291488 | tf_op jit(solution)/shard_map/ppermute | solution.py:65
  169.7 0.6 add.74
  170.3 0.0 copy-start.6
  170.3 0.0 copy-start.11
  170.3 1.9 collective-permute-start.2
  172.2 135.2 %collective-permute-done.2 = f32[24,65536]{1,0:T(8,128)S(1)} collective-permute-done((f32[24,65536]{1,0:T(8,128)S(1)}, f32[24,65536]{1,0:T(8,128)S(1)}, u32[]{:S(2)}, u32[]{:S(2)}) %collective-permute-start.2) | collective-permute-done | bytes 6291488 | tf_op jit(solution)/shard_map/ppermute | solution.py:65
  307.4 3.3 add.75
  310.6 2.5 collective-permute-start.3
  313.2 0.5 copy.31
  313.7 0.5 copy.32
  314.2 0.0 copy-start.2
  314.3 1.9 copy.33
  316.1 0.0 copy-start.4
  316.1 3.1 maximum_convert_fusion
  319.2 6.5 %copy.45 = f32[3,8,256,256]{3,2,1,0:T(8,128)} copy(f32[3,8,256,256]{2,3,1,0:T(8,128)} %maximum_convert_fusion) | data formatting | bytes 12582912 | tf_op jit(solution)/shard_map/convert_element_type | solution.py:83
  325.8 1.0 multiply_reduce_fusion
  326.8 0.0 copy-start.9
  326.8 0.0 copy-start.12
  326.8 2.4 copy.56
  329.9 1.7 fusion.47
  331.6 2.5 fusion.29
  334.0 1.3 copy.30
  335.4 1.0 copy.49
  336.4 246.4 %collective-permute-done.3 = f32[24,65536]{1,0:T(8,128)} collective-permute-done((f32[24,65536]{1,0:T(8,128)}, f32[24,65536]{1,0:T(8,128)}, u32[]{:S(2)}, u32[]{:S(2)}) %collective-permute-start.3) | collective-permute-done | bytes 6291488 | tf_op jit(solution)/shard_map/ppermute | solution.py:65
  582.8 5.4 multiply_reduce_fusion.1
  588.2 0.4 divide_convert_fusion.1
  588.6 0.7 copy.61
  589.4 2.7 fusion.74
  592.0 7.8 %add_convert_fusion.4 = bf16[24,256,256]{2,1,0:T(8,128)(2,1)} fusion(bf16[24,256,256]{2,1,0:T(8,128)(2,1)S(1)} %bitcast.116, bf16[24,256,256]{2,1,0:T(8,128)(2,1)} %fusion.74), kind=kOutput, calls=%fused_computation.10 | convolution fusion | flops 1624768512 | bytes 9437184 | tf_op jit(solution)/shard_map/mij,mjk->mik/dot_general | solution.py:79
  599.9 5.5 fusion.75
  605.4 8.1 %add_convert_fusion.2 = bf16[24,256,256]{2,1,0:T(8,128)(2,1)S(1)} fusion(bf16[24,256,256]{2,1,0:T(8,128)(2,1)} %add_convert_fusion.4, bf16[24,256,256]{2,1,0:T(8,128)(2,1)} %fusion.75), kind=kOutput, calls=%fused_computation.8 | convolution fusion | flops 1624768512 | bytes 9437184 | tf_op jit(solution)/shard_map/mij,mjk->mik/dot_general | solution.py:79
  613.6 2.7 fusion.76
  616.2 11.7 %fusion.1 = (f32[24,256]{1,0:T(8,128)S(1)}, f32[24,256,256]{2,1,0:T(8,128)}) fusion(f32[3,8,256,256]{3,2,1,0:T(8,128)} %copy.45, bf16[24,256,256]{2,1,0:T(8,128)(2,1)S(1)} %add_convert_fusion.2, bf16[24,256,256]{2,1,0:T(8,128)(2,1)} %fusion.76), kind=kOutput, calls=%fused_computation.3 | convolution fusion | flops 1631053824 | bytes 18898944 | tf_op jit(solution)/shard_map/mij,mjk->mik/dot_general | solution.py:79
  628.0 6.7 %copy.44 = f32[3,8,256,256]{2,3,1,0:T(8,128)} copy(f32[3,8,256,256]{3,2,1,0:T(8,128)} %bitcast.129) | data formatting | bytes 12582912 | tf_op jit(solution)/shard_map/convert_element_type | solution.py:84
  634.7 0.0 copy-start.13
  634.7 4.6 divide_convert_fusion
  639.3 0.0 copy-start.14
  639.3 1.6 copy-done.7
  640.9 0.0 copy-done.13
  640.9 0.4 fusion.31
  641.4 3.5 convolution_convert_fusion
  644.9 1.5 copy.48
  646.4 1.1 broadcast_select_fusion
  (22 shorter events, 0.1 us)
Async XLA Ops:
  0.6 1.9 copy-start.10
  0.6 3.2 copy-start.16
  0.7 3.4 copy-start.8
  0.7 3.4 copy-start.17
  4.5 1.0 copy-start.15
  16.8 10.5 %collective-permute-start = (f32[24,65536]{1,0:T(8,128)}, f32[24,65536]{1,0:T(8,128)S(1)}, u32[]{:S(2)}, u32[]{:S(2)}) collective-permute-start(f32[24,65536]{1,0:T(8,128)} %bitcast.117), channel_id=1, source_target_pairs={{0,1},{1,0},{2,3},{3,2},{4,5},{5,4},{6,7},{7,6},{8,9},{9,8},{10,11... | collective-permute-start | bytes 18874376 | tf_op jit(solution)/shard_map/ppermute | solution.py:65
  30.9 138.8 %collective-permute-start.1 = (f32[24,65536]{1,0:T(8,128)S(1)}, f32[24,65536]{1,0:T(8,128)S(1)}, u32[]{:S(2)}, u32[]{:S(2)}) collective-permute-start(f32[24,65536]{1,0:T(8,128)S(1)} %add.73), channel_id=1, source_target_pairs={{0,2},{1,3},{2,0},{3,1},{4,6},{5,7},{6,4},{7,5},{8,10},{9,11},{10,... | collective-permute-start | bytes 18874376 | tf_op jit(solution)/shard_map/ppermute | solution.py:65
  170.3 142.9 %copy-start.6 = (bf16[8,256,256]{2,1,0:T(8,128)(2,1)S(1)}, bf16[8,256,256]{2,1,0:T(8,128)(2,1)}, u32[]{:S(2)}) copy-start(bf16[8,256,256]{2,1,0:T(8,128)(2,1)} %param.13) | copy-start | bytes 3145732
  170.3 143.4 %copy-start.11 = (bf16[8,256,256]{2,1,0:T(8,128)(2,1)S(1)}, bf16[8,256,256]{2,1,0:T(8,128)(2,1)}, u32[]{:S(2)}) copy-start(bf16[8,256,256]{2,1,0:T(8,128)(2,1)} %param.14) | copy-start | bytes 3145732
  170.3 137.0 %collective-permute-start.2 = (f32[24,65536]{1,0:T(8,128)S(1)}, f32[24,65536]{1,0:T(8,128)S(1)}, u32[]{:S(2)}, u32[]{:S(2)}) collective-permute-start(f32[24,65536]{1,0:T(8,128)S(1)} %add.74), channel_id=1, source_target_pairs={{0,4},{1,5},{2,6},{3,7},{4,0},{5,1},{6,2},{7,3},{8,12},{9,13},{10,... | collective-permute-start | bytes 18874376 | tf_op jit(solution)/shard_map/ppermute | solution.py:65
  310.6 272.2 %collective-permute-start.3 = (f32[24,65536]{1,0:T(8,128)}, f32[24,65536]{1,0:T(8,128)}, u32[]{:S(2)}, u32[]{:S(2)}) collective-permute-start(f32[24,65536]{1,0:T(8,128)} %add.75), channel_id=1, source_target_pairs={{0,8},{1,9},{2,10},{3,11},{4,12},{5,13},{6,14},{7,15},{8,0},{9,1},... | collective-permute-start | bytes 18874376 | tf_op jit(solution)/shard_map/ppermute | solution.py:65
  313.7 12.0 %copy-start = (bf16[8,256,256]{1,2,0:T(8,128)(2,1)}, bf16[8,256,256]{1,2,0:T(8,128)(2,1)S(1)}, u32[]{:S(2)}) copy-start(bf16[8,256,256]{1,2,0:T(8,128)(2,1)S(1)} %copy.31) | copy-start | bytes 3145732
  314.2 11.5 %copy-start.2 = (bf16[8,256,256]{1,2,0:T(8,128)(2,1)}, bf16[8,256,256]{1,2,0:T(8,128)(2,1)S(1)}, u32[]{:S(2)}) copy-start(bf16[8,256,256]{1,2,0:T(8,128)(2,1)S(1)} %copy.32) | copy-start | bytes 3145732
  316.1 9.6 %copy-start.4 = (bf16[8,256,256]{1,2,0:T(8,128)(2,1)}, bf16[8,256,256]{1,2,0:T(8,128)(2,1)S(1)}, u32[]{:S(2)}) copy-start(bf16[8,256,256]{1,2,0:T(8,128)(2,1)S(1)} %copy.33) | copy-start | bytes 3145732
  326.8 4.8 copy-start.9
  326.8 4.8 copy-start.12
  627.9 6.7 %copy-start.1 = (bf16[8,256,256]{1,2,0:T(8,128)(2,1)S(1)}, bf16[8,256,256]{1,2,0:T(8,128)(2,1)}, u32[]{:S(2)}) copy-start(bf16[8,256,256]{1,2,0:T(8,128)(2,1)} %copy-done) | copy-start | bytes 3145732
  627.9 6.7 %copy-start.3 = (bf16[8,256,256]{1,2,0:T(8,128)(2,1)S(1)}, bf16[8,256,256]{1,2,0:T(8,128)(2,1)}, u32[]{:S(2)}) copy-start(bf16[8,256,256]{1,2,0:T(8,128)(2,1)} %copy-done.2) | copy-start | bytes 3145732
  627.9 6.7 %copy-start.5 = (bf16[8,256,256]{1,2,0:T(8,128)(2,1)S(1)}, bf16[8,256,256]{1,2,0:T(8,128)(2,1)}, u32[]{:S(2)}) copy-start(bf16[8,256,256]{1,2,0:T(8,128)(2,1)} %copy-done.4) | copy-start | bytes 3145732
  634.7 6.2 copy-start.13
  639.3 1.6 copy-start.7
  639.3 2.1 copy-start.14
